TPU v7x, 128 devices: a whole 4x4x4 slice. The times are simulated.
128 devices in a mesh: row: 16 (over y_hi, x, core), col: 8 (over z, y_lo).
Axes of the slice: x: 4, y: 4 (y_hi: 2, y_lo: 2; y = y_hi * 2 + y_lo), z: 4, core: 2. Of those that a mesh axis runs over, the one named last changes fastest.
Arguments:
- orbitals_in: float32 [16384, 256], P(('row', 'col')), may hold values from -6 to 6
- hblocks: bfloat16 [256, 128, 4096], P('row', 'col'), may hold values from -0.046875 to 0.046875
- block_cols: int32 [256, 128], P('row', 'col'), may hold values from 0 to 31, as said below
- live_counts: int32 [256, 8], P('row', 'col'), may hold values from 0 to 16, as said below
- onsite: bfloat16 [256, 4096], P(('row', 'col')), may hold values from -3 to 1, as said below
- cut_low: float32 [1], replicated, may hold values from -1.6 to -1
- top_bound: float32 [1], replicated, may hold values from 2.4 to 3.2
Outputs:
- orbitals: float32 [16384, 256], P(('row', 'col'))
- projected: float32 [256, 256], replicated
Inputs may be any that keep to these rules, and one draw needn't show every extreme that they name: `block_cols`: in block row b and column group c the first live_counts[b, c] slots name distinct block columns whose global block index exceeds b (strict upper triangle); the other slots are padding and are ignored. `live_counts`: block row 0 fills all 16 slots of every column group; the last block row has no live slot. `onsite`: every block is symmetric.
All inputs are finite; a program needn't handle non-finite values.
Results may differ from a plain program's by a relative error of at most 0.0008.
The roundings to bfloat16 on the way count: a program that leaves them out, or rounds other values in their place, can miss the bound.
Values may be sent and summed in bfloat16 or wider, within the bound.
A program may use at most 128 MiB of HBM per device.

v0:
```python
import jax
import jax.numpy as jnp
from jax import lax
from jax.sharding import PartitionSpec as P

BS = 64
K = 256
PB = 2
DEG = 3


def add_columns(dense_tile, portion):
    return jnp.dot(dense_tile, portion, preferred_element_type=jnp.float32)


def mirror_rows(dense_tile, row_set):
    return lax.dot_general(
        dense_tile, row_set, (((0,), (0,)), ((), ())), preferred_element_type=jnp.float32
    )


def build_tile(hblocks, block_cols, live_counts, column_blocks):
    row_blocks, slot_count, _ = hblocks.shape
    occupied = jnp.arange(slot_count, dtype=jnp.int32)[None, :] < live_counts
    selector = (
        block_cols[:, :, None] == jnp.arange(column_blocks, dtype=jnp.int32)[None, None, :]
    ) & occupied[:, :, None]
    blocks = hblocks.reshape(row_blocks, slot_count, BS, BS)
    dense_tile = jnp.einsum(
        "isc,isab->iacb", selector.astype(jnp.bfloat16), blocks, preferred_element_type=jnp.float32
    )
    return dense_tile.astype(jnp.bfloat16).reshape(row_blocks * BS, column_blocks * BS)


def local(orbitals_in, hblocks, block_cols, live_counts, onsite, cut_low, top_bound):
    row_devices = lax.axis_size("row")
    col_devices = lax.axis_size("col")
    column_blocks = row_devices * PB
    local_rows = PB * BS
    total_rows = row_devices * col_devices * local_rows
    dense_tile = build_tile(hblocks, block_cols, live_counts, column_blocks)
    onsite_blocks = onsite.reshape(PB, BS, BS)

    def reduce_direct(terms):
        return lax.psum_scatter(terms, "col", scatter_dimension=0, tiled=True)

    def apply(rounded):
        onsite_part = jnp.einsum(
            "pab,pbk->pak",
            onsite_blocks,
            rounded.reshape(PB, BS, K),
            preferred_element_type=jnp.float32,
        ).reshape(local_rows, K)
        direct = reduce_direct(
            add_columns(dense_tile, lax.all_gather(rounded, "row", axis=0, tiled=True))
        )
        mirror = lax.psum_scatter(
            mirror_rows(dense_tile, lax.all_gather(rounded, "col", axis=0, tiled=True)),
            "row",
            scatter_dimension=0,
            tiled=True,
        )
        return onsite_part + direct + mirror

    centre = 0.5 * (top_bound[0] + cut_low[0])
    halfwidth = 0.5 * (top_bound[0] - cut_low[0])
    previous = orbitals_in
    current = (apply(orbitals_in.astype(jnp.bfloat16)) - centre * orbitals_in) / halfwidth
    for degree in range(DEG - 1):
        following = (
            2.0 * (apply(current.astype(jnp.bfloat16)) - centre * current) / halfwidth - previous
        )
        previous, current = (current, following)
    rounded = current.astype(jnp.bfloat16)
    as_float = rounded.astype(jnp.float32)
    contract = (((0,), (0,)), ((), ()))
    gram_part = lax.dot_general(rounded, rounded, contract, preferred_element_type=jnp.float32)
    image = apply(rounded)
    cross_part = lax.dot_general(as_float, image, contract, precision=lax.Precision.HIGHEST)
    gram_total, cross_total = lax.psum((gram_part, cross_part), ("row", "col"))
    gram_matrix = gram_total / total_rows
    ritz_matrix = (cross_total + cross_total.T) / (2.0 * total_rows)
    factor = jnp.linalg.cholesky(gram_matrix)
    orbitals = jax.scipy.linalg.solve_triangular(factor, current.T, lower=True).T
    inner = jax.scipy.linalg.solve_triangular(factor, ritz_matrix, lower=True)
    projected = jax.scipy.linalg.solve_triangular(factor, inner.T, lower=True)
    return (orbitals, projected)


def solution(mesh):
    placed = (
        P(("row", "col"), None),
        P("row", "col", None),
        P("row", "col"),
        P("row", "col"),
        P(("row", "col"), None),
        P(),
        P(),
    )
    return jax.shard_map(
        local, mesh=mesh, in_specs=placed, out_specs=(P(("row", "col"), None), P()), check_vma=False
    )
```

profile of v0, /device:TPU:1, one launch (start us, length us, event | category | flops | bytes accessed | tf_op | source)
XLA Modules:
  0.0 903.4 jit_solution(17615895773485688638)
XLA Ops:
  7.2 1.5 convert_element_type.20
  8.8 6.9 reshape.92
  15.8 8.9 convert_bitcast_fusion
  24.7 12.4 %reshape.93 = bf16[1024,2048]{1,0:T(8,128)(2,1)} reshape(bf16[16,64,32,64]{3,2,1,0:T(8,128)(2,1)} %convert_bitcast_fusion) | data formatting | bytes 8388608 | tf_op jit(solution)/shard_map/reshape | solution.py:32
  37.1 29.5 %all_gather.25 = bf16[1024,256]{1,0:T(8,128)(2,1)S(1)} all-gather(bf16[128,256]{1,0:T(8,128)(2,1)S(1)} %copy-done.2), channel_id=1, replica_groups=mesh['row'=16,'col'=8] {'col'}, dimensions={0}, use_global_device_ids=true | all-gather | bytes 589824 | tf_op jit(solution)/shard_map/all_gather | solution.py:58
  66.6 4.8 fusion.46
  71.6 4.7 fusion.45
  77.9 67.4 %reduce-scatter.11.cloned.1.call-done = f32[128,256]{1,0:T(8,128)} async-done(((f32[2048,256]{1,0:T(8,128)}), f32[128,256]{1,0:T(8,128)}) %reduce-scatter.11.cloned.1.call-update) | async-done | bytes 131088 | tf_op jit(solution)/shard_map/reduce_scatter | solution.py:57
  145.3 39.7 %reduce-scatter.9.cloned.1.call-done = f32[128,256]{1,0:T(8,128)} async-done(((f32[1024,256]{1,0:T(8,128)}), f32[128,256]{1,0:T(8,128)}) %reduce-scatter.9.cloned.1.call-update) | async-done | bytes 131088 | tf_op jit(solution)/shard_map/reduce_scatter | solution.py:45
  185.0 1.6 fusion.41
  186.7 23.9 %all_gather.27 = bf16[1024,256]{1,0:T(8,128)(2,1)S(1)} all-gather(bf16[128,256]{1,0:T(8,128)(2,1)} %get-tuple-element.43), channel_id=1, replica_groups=mesh['row'=16,'col'=8] {'col'}, dimensions={0}, use_global_device_ids=true | all-gather | bytes 589824 | tf_op jit(solution)/shard_map/all_gather | solution.py:58
  210.7 4.8 fusion.48
  215.6 21.6 %all-gather.7.cloned.1.call-done = bf16[2048,256]{1,0:T(8,128)(2,1)} async-done(((bf16[128,256]{1,0:T(8,128)(2,1)}), bf16[2048,256]{1,0:T(8,128)(2,1)}) %all-gather.7.cloned.1.call-update) | async-done | bytes 1048592 | tf_op jit(solution)/shard_map/all_gather | solution.py:55
  237.2 4.7 fusion.47
  242.1 66.2 %reduce-scatter.15.cloned.1.call-done = f32[128,256]{1,0:T(8,128)} async-done(((f32[2048,256]{1,0:T(8,128)}), f32[128,256]{1,0:T(8,128)}) %reduce-scatter.15.cloned.1.call-update) | async-done | bytes 131088 | tf_op jit(solution)/shard_map/reduce_scatter | solution.py:57
  308.3 39.6 %reduce-scatter.13.cloned.1.call-done = f32[128,256]{1,0:T(8,128)} async-done(((f32[1024,256]{1,0:T(8,128)}), f32[128,256]{1,0:T(8,128)}) %reduce-scatter.13.cloned.1.call-update) | async-done | bytes 131088 | tf_op jit(solution)/shard_map/reduce_scatter | solution.py:45
  347.9 1.6 fusion.39
  349.7 24.2 %all_gather.29 = bf16[1024,256]{1,0:T(8,128)(2,1)S(1)} all-gather(bf16[128,256]{1,0:T(8,128)(2,1)} %get-tuple-element.41), channel_id=1, replica_groups=mesh['row'=16,'col'=8] {'col'}, dimensions={0}, use_global_device_ids=true | all-gather | bytes 589824 | tf_op jit(solution)/shard_map/all_gather | solution.py:58
  373.9 4.8 fusion.50
  378.8 21.2 %all-gather.9.cloned.1.call-done = bf16[2048,256]{1,0:T(8,128)(2,1)} async-done(((bf16[128,256]{1,0:T(8,128)(2,1)}), bf16[2048,256]{1,0:T(8,128)(2,1)}) %all-gather.9.cloned.1.call-update) | async-done | bytes 1048592 | tf_op jit(solution)/shard_map/all_gather | solution.py:55
  400.0 4.7 fusion.49
  405.0 66.3 %reduce-scatter.19.cloned.1.call-done = f32[128,256]{1,0:T(8,128)} async-done(((f32[2048,256]{1,0:T(8,128)}), f32[128,256]{1,0:T(8,128)}) %reduce-scatter.19.cloned.1.call-update) | async-done | bytes 131088 | tf_op jit(solution)/shard_map/reduce_scatter | solution.py:57
  471.3 39.7 %reduce-scatter.17.cloned.1.call-done = f32[128,256]{1,0:T(8,128)} async-done(((f32[1024,256]{1,0:T(8,128)}), f32[128,256]{1,0:T(8,128)}) %reduce-scatter.17.cloned.1.call-update) | async-done | bytes 131088 | tf_op jit(solution)/shard_map/reduce_scatter | solution.py:45
  511.0 1.6 fusion.37
  512.8 24.1 %all_gather.31 = bf16[1024,256]{1,0:T(8,128)(2,1)S(1)} all-gather(bf16[128,256]{1,0:T(8,128)(2,1)} %get-tuple-element.39), channel_id=1, replica_groups=mesh['row'=16,'col'=8] {'col'}, dimensions={0}, use_global_device_ids=true | all-gather | bytes 589824 | tf_op jit(solution)/shard_map/all_gather | solution.py:58
  536.8 4.8 fusion.53
  541.8 21.2 %all-gather.11.cloned.1.call-done = bf16[2048,256]{1,0:T(8,128)(2,1)} async-done(((bf16[128,256]{1,0:T(8,128)(2,1)}), bf16[2048,256]{1,0:T(8,128)(2,1)}) %all-gather.11.cloned.1.call-update) | async-done | bytes 1048592 | tf_op jit(solution)/shard_map/all_gather | solution.py:55
  563.0 4.7 fusion.52
  568.0 0.9 fusion.51
  568.9 65.4 %reduce-scatter.23.cloned.1.call-done = f32[128,256]{1,0:T(8,128)} async-done(((f32[2048,256]{1,0:T(8,128)}), f32[128,256]{1,0:T(8,128)}) %reduce-scatter.23.cloned.1.call-update) | async-done | bytes 131088 | tf_op jit(solution)/shard_map/reduce_scatter | solution.py:57
  634.3 39.6 %reduce-scatter.21.cloned.1.call-done = f32[128,256]{1,0:T(8,128)} async-done(((f32[1024,256]{1,0:T(8,128)}), f32[128,256]{1,0:T(8,128)}) %reduce-scatter.21.cloned.1.call-update) | async-done | bytes 131088 | tf_op jit(solution)/shard_map/reduce_scatter | solution.py:45
  673.9 1.0 fusion.7
  674.9 1.0 fusion.54
  675.9 152.6 %all-reduce.4.cloned.1.call-done = (f32[256,256]{0,1:T(8,128)}, f32[256,256]{1,0:T(8,128)}) async-done(((f32[256,256]{0,1:T(8,128)}, f32[256,256]{1,0:T(8,128)}), (f32[256,256]{0,1:T(8,128)}, f32[256,256]{1,0:T(8,128)})) %all-reduce.4.cloned.1.call-update) | async-done | bytes 524304 | tf_op jit(solution)/shard_map/psum | solution.py:80
  828.6 1.0 broadcast_multiply_fusion
  829.7 1.1 copy.12
  830.8 1.1 fusion.1
  831.9 11.7 %cholesky.50 = f32[128,128]{1,0:T(8,128)S(1)} custom-call(f32[128,128]{1,0:T(8,128)S(1)} %cholesky.118), custom_call_target="Cholesky" | custom-call | tf_op jit(solution)/shard_map/jit(cholesky)/cholesky | solution.py:83
  843.7 9.8 %custom-call.18 = f32[1,128,128]{1,2,0:T(8,128)S(1)} custom-call(f32[1,128,128]{2,1,0:T(8,128)S(1)} %get-tuple-element.50), custom_call_target="InvertDiagBlocksLowerTriangular" | custom-call | tf_op jit(solution)/shard_map/jit(cholesky)/cholesky | solution.py:83
  854.0 11.7 %cholesky.105 = f32[128,128]{1,0:T(8,128)S(1)} custom-call(f32[128,128]{1,0:T(8,128)S(1)} %convolution_subtract_fusion.3), custom_call_target="Cholesky" | custom-call | tf_op jit(solution)/shard_map/jit(cholesky)/cholesky | solution.py:83
  865.7 0.7 compare_reduce_fusion
  866.4 0.6 compare_reduce_fusion.1
  868.5 4.3 while.5
  869.3 1.4 bitcast_dynamic-update-slice_fusion.2
  871.4 1.4 bitcast_dynamic-update-slice_fusion.2
  872.8 19.7 %custom-call.19 = f32[2,128,128]{1,2,0:T(8,128)S(1)} custom-call(f32[2,128,128]{2,1,0:T(8,128)S(1)} %get-tuple-element.18), custom_call_target="InvertDiagBlocksLowerTriangular" | custom-call | tf_op jit(solution)/shard_map/jit(_solve_triangular)/triangular_solve | solution.py:84
  894.4 0.7 pad_maximum_fusion
  896.1 0.8 copy.13
  (75 shorter events, 6.3 us)
Async XLA Ops:
  7.2 8.6 copy-start.7
  7.2 8.7 copy-start.6
  7.2 64.4 %all-gather.5.cloned.1.call-start = ((), (), s32[]{:S(2)}) async-start(), calls=%async_computation.8 | async-start | bytes 1114112 | tf_op jit(solution)/shard_map/all_gather | solution.py:55
  8.8 136.5 %reduce-scatter.11.cloned.1.call-start = ((), (), s32[]{:S(2)}) async-start(), calls=%async_computation.10 | async-start | bytes 2228224 | tf_op jit(solution)/shard_map/reduce_scatter | solution.py:57
  24.7 12.4 %copy-start.2 = (bf16[128,256]{1,0:T(8,128)(2,1)S(1)}, bf16[128,256]{1,0:T(8,128)(2,1)}, u32[]{:S(2)}) copy-start(bf16[128,256]{1,0:T(8,128)(2,1)} %convert_element_type.20) | copy-start | bytes 196612
  71.5 6.2 copy-start.5
  71.5 113.6 %copy-start.1 = (f32[128,256]{1,0:T(8,128)S(1)}, f32[128,256]{1,0:T(8,128)}, u32[]{:S(2)}) copy-start(f32[128,256]{1,0:T(8,128)} %param.9) | copy-start | bytes 393220
  71.5 113.6 %reduce-scatter.9.cloned.1.call-start = ((), (), s32[]{:S(2)}) async-start(), calls=%async_computation.9 | async-start | bytes 1179648 | tf_op jit(solution)/shard_map/reduce_scatter | solution.py:45
  76.3 160.9 %all-gather.7.cloned.1.call-start = ((), (), s32[]{:S(2)}) async-start(), calls=%async_computation.11 | async-start | bytes 1114112 | tf_op jit(solution)/shard_map/all_gather | solution.py:55
  186.7 121.6 %reduce-scatter.15.cloned.1.call-start = ((), (), s32[]{:S(2)}) async-start(), calls=%async_computation.13 | async-start | bytes 2228224 | tf_op jit(solution)/shard_map/reduce_scatter | solution.py:57
  215.5 26.5 %copy-start.3 = (bf16[128,256]{1,0:T(8,128)(2,1)S(1)}, bf16[128,256]{1,0:T(8,128)(2,1)}, u32[]{:S(2)}) copy-start(bf16[128,256]{1,0:T(8,128)(2,1)} %get-tuple-element.43) | copy-start | bytes 196612
  215.5 132.4 %reduce-scatter.13.cloned.1.call-start = ((), (), s32[]{:S(2)}) async-start(), calls=%async_computation.12 | async-start | bytes 1179648 | tf_op jit(solution)/shard_map/reduce_scatter | solution.py:45
  241.9 158.1 %all-gather.9.cloned.1.call-start = ((), (), s32[]{:S(2)}) async-start(), calls=%async_computation.14 | async-start | bytes 1114112 | tf_op jit(solution)/shard_map/all_gather | solution.py:55
  349.6 121.7 %reduce-scatter.19.cloned.1.call-start = ((), (), s32[]{:S(2)}) async-start(), calls=%async_computation.16 | async-start | bytes 2228224 | tf_op jit(solution)/shard_map/reduce_scatter | solution.py:57
  378.7 26.1 %copy-start.4 = (bf16[128,256]{1,0:T(8,128)(2,1)S(1)}, bf16[128,256]{1,0:T(8,128)(2,1)}, u32[]{:S(2)}) copy-start(bf16[128,256]{1,0:T(8,128)(2,1)} %get-tuple-element.41) | copy-start | bytes 196612
  378.7 132.3 %reduce-scatter.17.cloned.1.call-start = ((), (), s32[]{:S(2)}) async-start(), calls=%async_computation.15 | async-start | bytes 1179648 | tf_op jit(solution)/shard_map/reduce_scatter | solution.py:45
  404.8 158.2 %all-gather.11.cloned.1.call-start = ((), (), s32[]{:S(2)}) async-start(), calls=%async_computation.17 | async-start | bytes 1114112 | tf_op jit(solution)/shard_map/all_gather | solution.py:55
  512.7 121.6 %reduce-scatter.23.cloned.1.call-start = ((), (), s32[]{:S(2)}) async-start(), calls=%async_computation.19 | async-start | bytes 2228224 | tf_op jit(solution)/shard_map/reduce_scatter | solution.py:57
  541.7 26.1 %copy-start = (bf16[128,256]{1,0:T(8,128)(2,1)S(1)}, bf16[128,256]{1,0:T(8,128)(2,1)}, u32[]{:S(2)}) copy-start(bf16[128,256]{1,0:T(8,128)(2,1)} %get-tuple-element.39) | copy-start | bytes 196612
  541.7 132.2 %reduce-scatter.21.cloned.1.call-start = ((), (), s32[]{:S(2)}) async-start(), calls=%async_computation.18 | async-start | bytes 1179648 | tf_op jit(solution)/shard_map/reduce_scatter | solution.py:45
  567.8 260.8 %all-reduce.4.cloned.1.call-start = ((), (), s32[]{:S(2)}) async-start(), calls=%async_computation.20 | async-start | bytes 1048576 | tf_op jit(solution)/shard_map/psum | solution.py:80
Sparse Core Ops, SparseCore 0:
  11.0 50.9 all-gather.4
  71.6 73.7 reduce-scatter.10
  147.7 37.2 reduce-scatter.8
  187.9 49.2 all-gather.6
  241.0 67.3 reduce-scatter.14
  310.6 37.3 reduce-scatter.12
  351.0 49.0 all-gather.8
  404.0 67.3 reduce-scatter.18
  473.7 37.2 reduce-scatter.16
  513.9 49.0 all-gather.10
  566.9 67.3 reduce-scatter.22
  636.5 37.3 reduce-scatter.20
  679.4 149.1 all-reduce.3
where the time goes:
time: 904 us; the launch traced here: 903 us
  waiting for transfers between devices  641 us (71%)
  blocking collectives  102 us (11%)
  other arithmetic  64.7 us (7%)
  matrix products  52.9 us (6%)
  local copies, waits for them, and re-layouts  25.5 us (3%)
  between operations  16.8 us (2%)
    reduce_scatter x4, waiting for transfers between devices, apply(): lax.psum_scatter(mirror_rows(dense_tile, lax.all_gather(rounded, 'col', a...  265 us
    reduce_scatter x4, waiting for transfers between devices, reduce_direct(): return lax.psum_scatter(terms, 'col', scatter_dimension=0, tiled=True)  159 us
    psum x1, waiting for transfers between devices, local(): gram_total, cross_total = lax.psum((gram_part, cross_part), ('row', 'col'))  153 us
    all_gather x4, blocking collectives, apply(): lax.all_gather(rounded, 'col', axis=0, tiled=True)  102 us
    all_gather x4, waiting for transfers between devices, apply(): lax.all_gather(rounded, 'row', axis=0, tiled=True)  64.1 us
    another operation x7, other arithmetic, local(): factor = jnp.linalg.cholesky(gram_matrix)  34.7 us
    another operation x3, other arithmetic, local(): jax.scipy.linalg.solve_triangular(factor, current.T, lower=True)  19.7 us
    dot_general x4, matrix products, mirror_rows(): lax.dot_general(dense_tile, row_set, (((0,), (0,)), ((), ())), preferred_...  19.4 us
  transfers between devices with their start and end apart: 13, of which 12 were waited for; matrix products, arithmetic and copies ran while one was open for 8% of the time, Pallas kernels for 0%

commit v1 on v0

--- a/solution.py
+++ b/solution.py
@@ -77,7 +77,7 @@
     gram_part = lax.dot_general(rounded, rounded, contract, preferred_element_type=jnp.float32)
     image = apply(rounded)
     cross_part = lax.dot_general(as_float, image, contract, precision=lax.Precision.HIGHEST)
-    gram_total, cross_total = lax.psum((gram_part, cross_part), ("row", "col"))
+    gram_total, cross_total = lax.psum(lax.psum((gram_part, cross_part), "col"), "row")
     gram_matrix = gram_total / total_rows
     ritz_matrix = (cross_total + cross_total.T) / (2.0 * total_rows)
     factor = jnp.linalg.cholesky(gram_matrix)

time: 904 us -> 973 us (1.076)
  waiting for transfers between devices: 641 us -> 710 us
    psum x1 -> x2, waiting for transfers between devices: 153 us -> 221 us  [the longest x1 145 us: local(): lax.psum(lax.psum((gram_part, cross_part), 'col'), 'row')]
  transfers between devices with their start and end apart: 13 -> 14, of which waited for: 12 -> 13; matrix products, arithmetic and copies ran while one was open for 8% -> 7% of each run, Pallas kernels for 0% -> 0%
where the time goes in v1:
time: 973 us; the launch traced here: 972 us
  waiting for transfers between devices  710 us (73%)
  blocking collectives  101 us (10%)
  other arithmetic  64.6 us (7%)
  matrix products  52.8 us (5%)
  local copies, waits for them, and re-layouts  25.4 us (3%)
  between operations  16.8 us (2%)
    reduce_scatter x4, waiting for transfers between devices, apply(): lax.psum_scatter(mirror_rows(dense_tile, lax.all_gather(rounded, 'col', a...  266 us
    reduce_scatter x4, waiting for transfers between devices, reduce_direct(): return lax.psum_scatter(terms, 'col', scatter_dimension=0, tiled=True)  159 us
    psum x1, waiting for transfers between devices, local(): lax.psum(lax.psum((gram_part, cross_part), 'col'), 'row')  145 us
    all_gather x4, blocking collectives, apply(): lax.all_gather(rounded, 'col', axis=0, tiled=True)  101 us
    psum x1, waiting for transfers between devices, local(): lax.psum((gram_part, cross_part), 'col')  76.2 us
    all_gather x4, waiting for transfers between devices, apply(): lax.all_gather(rounded, 'row', axis=0, tiled=True)  63.8 us
    another operation x7, other arithmetic, local(): factor = jnp.linalg.cholesky(gram_matrix)  34.6 us
    another operation x3, other arithmetic, local(): jax.scipy.linalg.solve_triangular(factor, current.T, lower=True)  19.7 us
  transfers between devices with their start and end apart: 14, of which 13 were waited for; matrix products, arithmetic and copies ran while one was open for 7% of the time, Pallas kernels for 0%

profile of v1, /device:TPU:1, one launch (start us, length us, event | category | flops | bytes accessed | tf_op | source)
XLA Modules:
  0.0 971.7 jit_solution(8816418691415318224)
XLA Ops:
  7.2 1.5 convert_element_type.20
  8.8 6.9 reshape.92
  15.8 8.9 convert_bitcast_fusion
  24.7 12.4 %reshape.93 = bf16[1024,2048]{1,0:T(8,128)(2,1)} reshape(bf16[16,64,32,64]{3,2,1,0:T(8,128)(2,1)} %convert_bitcast_fusion) | data formatting | bytes 8388608 | tf_op jit(solution)/shard_map/reshape | solution.py:32
  37.1 29.0 %all_gather.25 = bf16[1024,256]{1,0:T(8,128)(2,1)S(1)} all-gather(bf16[128,256]{1,0:T(8,128)(2,1)S(1)} %copy-done.2), channel_id=1, replica_groups=mesh['row'=16,'col'=8] {'col'}, dimensions={0}, use_global_device_ids=true | all-gather | bytes 589824 | tf_op jit(solution)/shard_map/all_gather | solution.py:58
  66.1 4.8 fusion.46
  71.1 4.7 fusion.45
  77.4 67.9 %reduce-scatter.11.cloned.1.call-done = f32[128,256]{1,0:T(8,128)} async-done(((f32[2048,256]{1,0:T(8,128)}), f32[128,256]{1,0:T(8,128)}) %reduce-scatter.11.cloned.1.call-update) | async-done | bytes 131088 | tf_op jit(solution)/shard_map/reduce_scatter | solution.py:57
  145.4 39.9 %reduce-scatter.9.cloned.1.call-done = f32[128,256]{1,0:T(8,128)} async-done(((f32[1024,256]{1,0:T(8,128)}), f32[128,256]{1,0:T(8,128)}) %reduce-scatter.9.cloned.1.call-update) | async-done | bytes 131088 | tf_op jit(solution)/shard_map/reduce_scatter | solution.py:45
  185.2 1.6 fusion.41
  186.9 24.0 %all_gather.27 = bf16[1024,256]{1,0:T(8,128)(2,1)S(1)} all-gather(bf16[128,256]{1,0:T(8,128)(2,1)} %get-tuple-element.45), channel_id=1, replica_groups=mesh['row'=16,'col'=8] {'col'}, dimensions={0}, use_global_device_ids=true | all-gather | bytes 589824 | tf_op jit(solution)/shard_map/all_gather | solution.py:58
  210.9 4.8 fusion.48
  215.9 21.3 %all-gather.7.cloned.1.call-done = bf16[2048,256]{1,0:T(8,128)(2,1)} async-done(((bf16[128,256]{1,0:T(8,128)(2,1)}), bf16[2048,256]{1,0:T(8,128)(2,1)}) %all-gather.7.cloned.1.call-update) | async-done | bytes 1048592 | tf_op jit(solution)/shard_map/all_gather | solution.py:55
  237.1 4.7 fusion.47
  242.1 66.2 %reduce-scatter.15.cloned.1.call-done = f32[128,256]{1,0:T(8,128)} async-done(((f32[2048,256]{1,0:T(8,128)}), f32[128,256]{1,0:T(8,128)}) %reduce-scatter.15.cloned.1.call-update) | async-done | bytes 131088 | tf_op jit(solution)/shard_map/reduce_scatter | solution.py:57
  308.3 39.5 %reduce-scatter.13.cloned.1.call-done = f32[128,256]{1,0:T(8,128)} async-done(((f32[1024,256]{1,0:T(8,128)}), f32[128,256]{1,0:T(8,128)}) %reduce-scatter.13.cloned.1.call-update) | async-done | bytes 131088 | tf_op jit(solution)/shard_map/reduce_scatter | solution.py:45
  347.8 1.6 fusion.39
  349.5 24.3 %all_gather.29 = bf16[1024,256]{1,0:T(8,128)(2,1)S(1)} all-gather(bf16[128,256]{1,0:T(8,128)(2,1)} %get-tuple-element.43), channel_id=1, replica_groups=mesh['row'=16,'col'=8] {'col'}, dimensions={0}, use_global_device_ids=true | all-gather | bytes 589824 | tf_op jit(solution)/shard_map/all_gather | solution.py:58
  373.8 4.8 fusion.50
  378.7 21.2 %all-gather.9.cloned.1.call-done = bf16[2048,256]{1,0:T(8,128)(2,1)} async-done(((bf16[128,256]{1,0:T(8,128)(2,1)}), bf16[2048,256]{1,0:T(8,128)(2,1)}) %all-gather.9.cloned.1.call-update) | async-done | bytes 1048592 | tf_op jit(solution)/shard_map/all_gather | solution.py:55
  400.0 4.7 fusion.49
  404.9 66.4 %reduce-scatter.19.cloned.1.call-done = f32[128,256]{1,0:T(8,128)} async-done(((f32[2048,256]{1,0:T(8,128)}), f32[128,256]{1,0:T(8,128)}) %reduce-scatter.19.cloned.1.call-update) | async-done | bytes 131088 | tf_op jit(solution)/shard_map/reduce_scatter | solution.py:57
  471.3 39.7 %reduce-scatter.17.cloned.1.call-done = f32[128,256]{1,0:T(8,128)} async-done(((f32[1024,256]{1,0:T(8,128)}), f32[128,256]{1,0:T(8,128)}) %reduce-scatter.17.cloned.1.call-update) | async-done | bytes 131088 | tf_op jit(solution)/shard_map/reduce_scatter | solution.py:45
  511.0 1.6 fusion.37
  512.7 24.1 %all_gather.31 = bf16[1024,256]{1,0:T(8,128)(2,1)S(1)} all-gather(bf16[128,256]{1,0:T(8,128)(2,1)} %get-tuple-element.41), channel_id=1, replica_groups=mesh['row'=16,'col'=8] {'col'}, dimensions={0}, use_global_device_ids=true | all-gather | bytes 589824 | tf_op jit(solution)/shard_map/all_gather | solution.py:58
  536.8 4.8 fusion.53
  541.7 21.2 %all-gather.11.cloned.1.call-done = bf16[2048,256]{1,0:T(8,128)(2,1)} async-done(((bf16[128,256]{1,0:T(8,128)(2,1)}), bf16[2048,256]{1,0:T(8,128)(2,1)}) %all-gather.11.cloned.1.call-update) | async-done | bytes 1048592 | tf_op jit(solution)/shard_map/all_gather | solution.py:55
  562.9 4.7 fusion.52
  567.9 0.9 fusion.51
  568.8 65.4 %reduce-scatter.23.cloned.1.call-done = f32[128,256]{1,0:T(8,128)} async-done(((f32[2048,256]{1,0:T(8,128)}), f32[128,256]{1,0:T(8,128)}) %reduce-scatter.23.cloned.1.call-update) | async-done | bytes 131088 | tf_op jit(solution)/shard_map/reduce_scatter | solution.py:57
  634.2 39.6 %reduce-scatter.21.cloned.1.call-done = f32[128,256]{1,0:T(8,128)} async-done(((f32[1024,256]{1,0:T(8,128)}), f32[128,256]{1,0:T(8,128)}) %reduce-scatter.21.cloned.1.call-update) | async-done | bytes 131088 | tf_op jit(solution)/shard_map/reduce_scatter | solution.py:45
  673.8 1.0 fusion.7
  674.8 1.0 fusion.54
  675.9 76.2 %all-reduce.8.cloned.1.call-done = (f32[256,256]{0,1:T(8,128)}, f32[256,256]{1,0:T(8,128)}) async-done(((f32[256,256]{0,1:T(8,128)}, f32[256,256]{1,0:T(8,128)}), (f32[256,256]{0,1:T(8,128)}, f32[256,256]{1,0:T(8,128)})) %all-reduce.8.cloned.1.call-update) | async-done | bytes 524304 | tf_op jit(solution)/shard_map/psum | solution.py:80
  752.1 145.0 %all-reduce.6.cloned.1.call-done = (f32[256,256]{0,1:T(8,128)}, f32[256,256]{1,0:T(8,128)}) async-done(((f32[256,256]{0,1:T(8,128)}, f32[256,256]{1,0:T(8,128)}), (f32[256,256]{0,1:T(8,128)}, f32[256,256]{1,0:T(8,128)})) %all-reduce.6.cloned.1.call-update) | async-done | bytes 524304 | tf_op jit(solution)/shard_map/psum | solution.py:80
  897.2 1.0 broadcast_multiply_fusion
  898.3 1.1 copy.12
  899.4 1.1 fusion.1
  900.5 11.7 %cholesky.50 = f32[128,128]{1,0:T(8,128)S(1)} custom-call(f32[128,128]{1,0:T(8,128)S(1)} %cholesky.118), custom_call_target="Cholesky" | custom-call | tf_op jit(solution)/shard_map/jit(cholesky)/cholesky | solution.py:83
  912.3 9.8 %custom-call.18 = f32[1,128,128]{1,2,0:T(8,128)S(1)} custom-call(f32[1,128,128]{2,1,0:T(8,128)S(1)} %get-tuple-element.52), custom_call_target="InvertDiagBlocksLowerTriangular" | custom-call | tf_op jit(solution)/shard_map/jit(cholesky)/cholesky | solution.py:83
  922.5 11.7 %cholesky.105 = f32[128,128]{1,0:T(8,128)S(1)} custom-call(f32[128,128]{1,0:T(8,128)S(1)} %convolution_subtract_fusion.3), custom_call_target="Cholesky" | custom-call | tf_op jit(solution)/shard_map/jit(cholesky)/cholesky | solution.py:83
  934.3 0.7 compare_reduce_fusion
  937.0 4.1 while.5
  937.7 1.4 bitcast_dynamic-update-slice_fusion.2
  939.7 1.4 bitcast_dynamic-update-slice_fusion.2
  941.1 19.7 %custom-call.19 = f32[2,128,128]{1,2,0:T(8,128)S(1)} custom-call(f32[2,128,128]{2,1,0:T(8,128)S(1)} %get-tuple-element.18), custom_call_target="InvertDiagBlocksLowerTriangular" | custom-call | tf_op jit(solution)/shard_map/jit(_solve_triangular)/triangular_solve | solution.py:84
  962.7 0.7 pad_maximum_fusion
  964.4 0.8 copy.13
  (78 shorter events, 7.0 us)
Async XLA Ops:
  7.2 8.6 copy-start.7
  7.2 8.7 copy-start.6
  7.2 63.9 %all-gather.5.cloned.1.call-start = ((), (), s32[]{:S(2)}) async-start(), calls=%async_computation.8 | async-start | bytes 1114112 | tf_op jit(solution)/shard_map/all_gather | solution.py:55
  8.8 136.6 %reduce-scatter.11.cloned.1.call-start = ((), (), s32[]{:S(2)}) async-start(), calls=%async_computation.10 | async-start | bytes 2228224 | tf_op jit(solution)/shard_map/reduce_scatter | solution.py:57
  24.7 12.4 %copy-start.2 = (bf16[128,256]{1,0:T(8,128)(2,1)S(1)}, bf16[128,256]{1,0:T(8,128)(2,1)}, u32[]{:S(2)}) copy-start(bf16[128,256]{1,0:T(8,128)(2,1)} %convert_element_type.20) | copy-start | bytes 196612
  71.0 6.2 copy-start.5
  71.0 114.2 %copy-start.1 = (f32[128,256]{1,0:T(8,128)S(1)}, f32[128,256]{1,0:T(8,128)}, u32[]{:S(2)}) copy-start(f32[128,256]{1,0:T(8,128)} %param.9) | copy-start | bytes 393220
  71.0 114.2 %reduce-scatter.9.cloned.1.call-start = ((), (), s32[]{:S(2)}) async-start(), calls=%async_computation.9 | async-start | bytes 1179648 | tf_op jit(solution)/shard_map/reduce_scatter | solution.py:45
  75.8 161.3 %all-gather.7.cloned.1.call-start = ((), (), s32[]{:S(2)}) async-start(), calls=%async_computation.11 | async-start | bytes 1114112 | tf_op jit(solution)/shard_map/all_gather | solution.py:55
  186.9 121.4 %reduce-scatter.15.cloned.1.call-start = ((), (), s32[]{:S(2)}) async-start(), calls=%async_computation.13 | async-start | bytes 2228224 | tf_op jit(solution)/shard_map/reduce_scatter | solution.py:57
  215.8 26.1 %copy-start.3 = (bf16[128,256]{1,0:T(8,128)(2,1)S(1)}, bf16[128,256]{1,0:T(8,128)(2,1)}, u32[]{:S(2)}) copy-start(bf16[128,256]{1,0:T(8,128)(2,1)} %get-tuple-element.45) | copy-start | bytes 196612
  215.8 132.0 %reduce-scatter.13.cloned.1.call-start = ((), (), s32[]{:S(2)}) async-start(), calls=%async_computation.12 | async-start | bytes 1179648 | tf_op jit(solution)/shard_map/reduce_scatter | solution.py:45
  241.9 158.1 %all-gather.9.cloned.1.call-start = ((), (), s32[]{:S(2)}) async-start(), calls=%async_computation.14 | async-start | bytes 1114112 | tf_op jit(solution)/shard_map/all_gather | solution.py:55
  349.5 121.8 %reduce-scatter.19.cloned.1.call-start = ((), (), s32[]{:S(2)}) async-start(), calls=%async_computation.16 | async-start | bytes 2228224 | tf_op jit(solution)/shard_map/reduce_scatter | solution.py:57
  378.7 26.1 %copy-start.4 = (bf16[128,256]{1,0:T(8,128)(2,1)S(1)}, bf16[128,256]{1,0:T(8,128)(2,1)}, u32[]{:S(2)}) copy-start(bf16[128,256]{1,0:T(8,128)(2,1)} %get-tuple-element.43) | copy-start | bytes 196612
  378.7 132.3 %reduce-scatter.17.cloned.1.call-start = ((), (), s32[]{:S(2)}) async-start(), calls=%async_computation.15 | async-start | bytes 1179648 | tf_op jit(solution)/shard_map/reduce_scatter | solution.py:45
  404.7 158.2 %all-gather.11.cloned.1.call-start = ((), (), s32[]{:S(2)}) async-start(), calls=%async_computation.17 | async-start | bytes 1114112 | tf_op jit(solution)/shard_map/all_gather | solution.py:55
  512.6 121.6 %reduce-scatter.23.cloned.1.call-start = ((), (), s32[]{:S(2)}) async-start(), calls=%async_computation.19 | async-start | bytes 2228224 | tf_op jit(solution)/shard_map/reduce_scatter | solution.py:57
  541.6 26.1 %copy-start = (bf16[128,256]{1,0:T(8,128)(2,1)S(1)}, bf16[128,256]{1,0:T(8,128)(2,1)}, u32[]{:S(2)}) copy-start(bf16[128,256]{1,0:T(8,128)(2,1)} %get-tuple-element.41) | copy-start | bytes 196612
  541.6 132.2 %reduce-scatter.21.cloned.1.call-start = ((), (), s32[]{:S(2)}) async-start(), calls=%async_computation.18 | async-start | bytes 1179648 | tf_op jit(solution)/shard_map/reduce_scatter | solution.py:45
  567.7 184.4 %all-reduce.8.cloned.1.call-start = ((), (), s32[]{:S(2)}) async-start(), calls=%async_computation.21 | async-start | bytes 1048576 | tf_op jit(solution)/shard_map/psum | solution.py:80
  675.9 221.3 %all-reduce.6.cloned.1.call-start = ((), (), s32[]{:S(2)}) async-start(), calls=%async_computation.20 | async-start | bytes 1048576 | tf_op jit(solution)/shard_map/psum | solution.py:80
Sparse Core Ops, SparseCore 0:
  11.0 50.9 all-gather.4
  71.1 74.2 reduce-scatter.10
  147.7 37.4 reduce-scatter.8
  188.1 48.9 all-gather.6
  240.9 67.3 reduce-scatter.14
  310.5 37.2 reduce-scatter.12
  350.8 49.0 all-gather.8
  403.9 67.3 reduce-scatter.18
  473.7 37.2 reduce-scatter.16
  513.9 49.0 all-gather.10
  566.9 67.3 reduce-scatter.22
  636.5 37.3 reduce-scatter.20
  676.9 75.1 all-reduce.7
  754.6 142.5 all-reduce.5
